TPU v7x, 32 devices: a whole 2x2x4 slice. The times are simulated.
32 devices in a mesh: wide: 16 (over z, y, core), narrow: 2 (over x).
Axes of the slice: x: 2, y: 2, z: 4, core: 2. Of those that a mesh axis runs over, the one named last changes fastest.
Arguments:
- inputs: bfloat16 [2, 32, 128, 1024], P(None, ('wide', 'narrow')), may hold values from -6 to 6
- out_grad: bfloat16 [2, 32, 128, 1024], P(None, ('wide', 'narrow')), may hold values from -6 to 6
- group_id: int32 [2, 32], P(None, ('wide', 'narrow')), may hold values from 0 to 15
- group_count: int32 [16], replicated, may hold values from 1 to 4
- norm_gain: bfloat16 [4, 1024], P(None, 'narrow'), may hold values from 0.5 to 1.5
- norm_bias: bfloat16 [4, 1024], P(None, 'narrow'), may hold values from -1.25 to 1.25
- w_qkv: bfloat16 [1024, 3072], P('narrow'), may hold values from -0.1875 to 0.1875
- w_out: bfloat16 [1024, 1024], P('narrow'), may hold values from -1.5 to 1.5
- w_up: bfloat16 [1024, 4096], P('narrow'), may hold values from -0.1875 to 0.1875
- w_down: bfloat16 [4096, 1024], P('narrow'), may hold values from -0.09375 to 0.09375
- bias_model: bfloat16 [4, 1024], P(None, 'narrow'), may hold values from -0.625 to 0.625
- bias_up: bfloat16 [4096], P('narrow'), may hold values from -0.625 to 0.625
Outputs:
- output: bfloat16 [2, 32, 128, 1024], P(None, ('wide', 'narrow'))
- grad_input: bfloat16 [2, 32, 128, 1024], P(None, ('wide', 'narrow'))
- grad_norm_gain: float32 [4, 1024], P(None, 'narrow')
- grad_norm_bias: float32 [4, 1024], P(None, 'narrow')
- grad_qkv: float32 [1024, 3072], P('narrow')
- grad_out: float32 [1024, 1024], P('narrow')
- grad_up: float32 [1024, 4096], P('narrow')
- grad_down: float32 [4096, 1024], P('narrow')
- grad_bias_model: float32 [4, 1024], P(None, 'narrow')
- grad_bias_up: float32 [4096], P('narrow')
All inputs are finite; a program needn't handle non-finite values.
Results may differ from a plain program's by a relative error of at most 0.02.
Values may be sent and summed in bfloat16 or wider, within the bound.
No kernel may reach another device: no remote copies, remote signals or barrier semaphores. Data moves between devices by JAX's collectives and lax.ppermute only.
A program may use at most 256 MiB of HBM per device.

v0:
```python
import math
import jax
import jax.numpy as jnp
from jax import lax
from jax.sharding import PartitionSpec as P

HEADS = 16
EPSILON = 1e-05
RELAX = 32.0


def layer_norm(value, gain, shift):
    average = jnp.mean(value, axis=-1, keepdims=True)
    centred = value - average
    spread = jnp.mean(centred * centred, axis=-1, keepdims=True)
    return centred * lax.rsqrt(spread + EPSILON) * gain + shift


def exact_gelu(value):
    return jax.nn.gelu(value, approximate=False)


def forward_product(left, right):
    return jnp.dot(left, right, preferred_element_type=jnp.float32)


def back_product(grad, weight):
    return lax.dot_general(
        grad, weight, (((1,), (1,)), ((), ())), preferred_element_type=jnp.float32
    )


def weight_grad(left, grad):
    return lax.dot_general(left, grad, (((0,), (0,)), ((), ())), preferred_element_type=jnp.float32)


def column_sum(grad):
    return jnp.sum(grad.astype(jnp.float32), axis=0)


def split_heads(qkv, seqs, heads):
    length = qkv.shape[0] // seqs
    width = qkv.shape[1] // 3
    parts = qkv.reshape(seqs, length, 3, heads, width // heads)
    return (parts[:, :, 0], parts[:, :, 1], parts[:, :, 2])


def raw_scores(query, keys):
    length = query.shape[1]
    scale = RELAX * math.sqrt(query.shape[-1])
    scores = jnp.einsum("sqhd,skhd->shqk", query, keys, preferred_element_type=jnp.float32) / scale
    rows = lax.broadcasted_iota(jnp.int32, (length, length), 0)
    columns = lax.broadcasted_iota(jnp.int32, (length, length), 1)
    return jnp.where(columns <= rows, scores, -1000000000.0)


def forward_pass(block, full, seqs, heads):
    gain = full[0].astype(jnp.float32)
    shift = full[1].astype(jnp.float32)
    bias = full[6].astype(jnp.float32)
    bias_hidden = full[7].astype(jnp.float32)
    tokens, width = block.shape
    qkv_bias = jnp.concatenate([bias[0], jnp.zeros((width,), jnp.float32), bias[1]])
    block_value = block.astype(jnp.float32)
    first = layer_norm(block_value, gain[0], shift[0]).astype(jnp.bfloat16)
    qkv = (forward_product(first, full[2]) + qkv_bias).astype(jnp.bfloat16)
    query, keys, values = split_heads(qkv, seqs, heads)
    scores = raw_scores(query, keys)
    top = jnp.max(scores, axis=-1, keepdims=True)
    exps = jnp.exp(RELAX * (scores - top))
    total = jnp.sum(exps, axis=-1, keepdims=True)
    logsum = jnp.log(total)
    weights = (exps / total).astype(jnp.bfloat16)
    mixed = jnp.einsum("shqk,skhd->sqhd", weights, values, preferred_element_type=jnp.float32)
    mixed = mixed.reshape(tokens, width).astype(jnp.bfloat16)
    branch = forward_product(mixed, full[3]) + bias[2]
    middle = block_value + layer_norm(branch, gain[1], shift[1])
    third = layer_norm(middle, gain[2], shift[2]).astype(jnp.bfloat16)
    hidden = forward_product(third, full[4]) + bias_hidden
    active = exact_gelu(hidden).astype(jnp.bfloat16)
    second = forward_product(active, full[5]) + bias[3]
    result = middle + layer_norm(second, gain[3], shift[3])
    kept = (
        block_value,
        first,
        qkv,
        top,
        logsum,
        mixed,
        branch,
        middle,
        third,
        hidden,
        active,
        second,
    )
    return (result, kept)


def attention_back(qkv, top, logsum, grad_mixed, seqs, heads):
    query, keys, values = split_heads(qkv, seqs, heads)
    scores = raw_scores(query, keys)
    probs = jnp.exp(RELAX * (scores - top) - logsum)
    weights = probs.astype(jnp.bfloat16)
    tokens, width = grad_mixed.shape
    grad_heads = grad_mixed.reshape(seqs, tokens // seqs, heads, width // heads)
    grad_weights = jnp.einsum(
        "sqhd,skhd->shqk", grad_heads, values, preferred_element_type=jnp.float32
    )
    inner = jnp.sum(probs * grad_weights, axis=-1, keepdims=True)
    grad_scores = (RELAX * probs * (grad_weights - inner)).astype(jnp.bfloat16)
    scale = RELAX * math.sqrt(query.shape[-1])
    grad_query = (
        jnp.einsum("shqk,skhd->sqhd", grad_scores, keys, preferred_element_type=jnp.float32) / scale
    )
    grad_keys = (
        jnp.einsum("shqk,sqhd->skhd", grad_scores, query, preferred_element_type=jnp.float32)
        / scale
    )
    grad_values = jnp.einsum(
        "shqk,sqhd->skhd", weights, grad_heads, preferred_element_type=jnp.float32
    )
    stacked = jnp.stack([grad_query, grad_keys, grad_values], axis=2)
    return stacked.reshape(tokens, 3 * width).astype(jnp.bfloat16)


def backward_pass(cotangent, full, kept, seqs, heads):
    block_value, first, qkv, top, logsum, mixed, branch, middle, third, hidden, active, second = (
        kept
    )
    gain = full[0].astype(jnp.float32)
    shift = full[1].astype(jnp.float32)
    width = block_value.shape[1]
    unused_last, pull_last = jax.vjp(layer_norm, second, gain[3], shift[3])
    grad_second, gain_last, shift_last = pull_last(cotangent)
    grad_second = grad_second.astype(jnp.bfloat16)
    grad_down = weight_grad(active, grad_second)
    bias_down = column_sum(grad_second)
    grad_active = back_product(grad_second, full[5])
    unused_gelu, pull_gelu = jax.vjp(exact_gelu, hidden)
    grad_hidden = pull_gelu(grad_active)[0].astype(jnp.bfloat16)
    grad_up = weight_grad(third, grad_hidden)
    bias_hidden = column_sum(grad_hidden)
    grad_third = back_product(grad_hidden, full[4])
    unused_third, pull_third = jax.vjp(layer_norm, middle, gain[2], shift[2])
    grad_inner, gain_third, shift_third = pull_third(grad_third)
    grad_middle = cotangent + grad_inner
    unused_branch, pull_branch = jax.vjp(layer_norm, branch, gain[1], shift[1])
    grad_branch, gain_branch, shift_branch = pull_branch(grad_middle)
    grad_branch = grad_branch.astype(jnp.bfloat16)
    grad_out = weight_grad(mixed, grad_branch)
    bias_out = column_sum(grad_branch)
    grad_mixed = back_product(grad_branch, full[3]).astype(jnp.bfloat16)
    grad_qkv = attention_back(qkv, top, logsum, grad_mixed, seqs, heads)
    grad_project = weight_grad(first, grad_qkv)
    qkv_sums = column_sum(grad_qkv)
    grad_first = back_product(grad_qkv, full[2])
    unused_first, pull_first = jax.vjp(layer_norm, block_value, gain[0], shift[0])
    grad_block, gain_first, shift_first = pull_first(grad_first)
    grad_input = grad_middle + grad_block
    grad_gain = jnp.stack([gain_first, gain_branch, gain_third, gain_last])
    grad_shift = jnp.stack([shift_first, shift_branch, shift_third, shift_last])
    grad_bias = jnp.stack([qkv_sums[:width], qkv_sums[2 * width :], bias_out, bias_down])
    return (
        grad_input,
        (grad_gain, grad_shift, grad_project, grad_out, grad_up, grad_down, grad_bias, bias_hidden),
    )


def on_device(
    inputs,
    out_grad,
    group_id,
    group_count,
    norm_gain,
    norm_bias,
    w_qkv,
    w_out,
    w_up,
    w_down,
    bias_model,
    bias_up,
):
    micros, seqs, length, width = inputs.shape
    heads = HEADS
    tokens = seqs * length
    matches = (
        group_id[:, :, None] == jnp.arange(group_count.shape[0], dtype=jnp.int32)[None, None, :]
    )
    counts = jnp.sum(jnp.where(matches, group_count[None, None, :], 0), axis=-1)
    seq_scale = 1.0 / counts.astype(jnp.float32)
    results = []
    grad_inputs = []
    totals = None
    for micro in range(micros):
        full = (
            lax.all_gather(norm_gain, "narrow", axis=1, tiled=True),
            lax.all_gather(norm_bias, "narrow", axis=1, tiled=True),
            lax.all_gather(w_qkv, "narrow", axis=0, tiled=True),
            lax.all_gather(w_out, "narrow", axis=0, tiled=True),
            lax.all_gather(w_up, "narrow", axis=0, tiled=True),
            lax.all_gather(w_down, "narrow", axis=0, tiled=True),
            lax.all_gather(bias_model, "narrow", axis=1, tiled=True),
            lax.all_gather(bias_up, "narrow", axis=0, tiled=True),
        )
        result, kept = forward_pass(inputs[micro].reshape(tokens, width), full, seqs, heads)
        results.append(result.reshape(seqs, length, width).astype(jnp.bfloat16))
        full = (
            lax.all_gather(norm_gain, "narrow", axis=1, tiled=True),
            lax.all_gather(norm_bias, "narrow", axis=1, tiled=True),
            lax.all_gather(w_qkv, "narrow", axis=0, tiled=True),
            lax.all_gather(w_out, "narrow", axis=0, tiled=True),
            lax.all_gather(w_up, "narrow", axis=0, tiled=True),
            lax.all_gather(w_down, "narrow", axis=0, tiled=True),
            lax.all_gather(bias_model, "narrow", axis=1, tiled=True),
            lax.all_gather(bias_up, "narrow", axis=0, tiled=True),
        )
        cotangent = out_grad[micro].astype(jnp.float32) * seq_scale[micro][:, None, None]
        grad_input, grads = backward_pass(cotangent.reshape(tokens, width), full, kept, seqs, heads)
        grad_inputs.append(grad_input.reshape(seqs, length, width).astype(jnp.bfloat16))
        shares = (
            lax.psum_scatter(
                grads[0].astype(jnp.bfloat16), "narrow", scatter_dimension=1, tiled=True
            ).astype(jnp.float32),
            lax.psum_scatter(
                grads[1].astype(jnp.bfloat16), "narrow", scatter_dimension=1, tiled=True
            ).astype(jnp.float32),
            lax.psum_scatter(
                grads[2].astype(jnp.bfloat16), "narrow", scatter_dimension=0, tiled=True
            ).astype(jnp.float32),
            lax.psum_scatter(
                grads[3].astype(jnp.bfloat16), "narrow", scatter_dimension=0, tiled=True
            ).astype(jnp.float32),
            lax.psum_scatter(
                grads[4].astype(jnp.bfloat16), "narrow", scatter_dimension=0, tiled=True
            ).astype(jnp.float32),
            lax.psum_scatter(
                grads[5].astype(jnp.bfloat16), "narrow", scatter_dimension=0, tiled=True
            ).astype(jnp.float32),
            lax.psum_scatter(
                grads[6].astype(jnp.bfloat16), "narrow", scatter_dimension=1, tiled=True
            ).astype(jnp.float32),
            lax.psum_scatter(
                grads[7].astype(jnp.bfloat16), "narrow", scatter_dimension=0, tiled=True
            ).astype(jnp.float32),
        )
        if totals is None:
            totals = tuple(shares)
        else:
            totals = tuple((left + right for left, right in zip(totals, shares)))
    summed = (
        lax.psum(totals[0].astype(jnp.bfloat16), "wide").astype(jnp.float32),
        lax.psum(totals[1].astype(jnp.bfloat16), "wide").astype(jnp.float32),
        lax.psum(totals[2].astype(jnp.bfloat16), "wide").astype(jnp.float32),
        lax.psum(totals[3].astype(jnp.bfloat16), "wide").astype(jnp.float32),
        lax.psum(totals[4].astype(jnp.bfloat16), "wide").astype(jnp.float32),
        lax.psum(totals[5].astype(jnp.bfloat16), "wide").astype(jnp.float32),
        lax.psum(totals[6].astype(jnp.bfloat16), "wide").astype(jnp.float32),
        lax.psum(totals[7].astype(jnp.bfloat16), "wide").astype(jnp.float32),
    )
    output = jnp.stack(results)
    grad_all = jnp.stack(grad_inputs)
    return (
        output,
        grad_all,
        summed[0],
        summed[1],
        summed[2],
        summed[3],
        summed[4],
        summed[5],
        summed[6],
        summed[7],
    )


def solution(mesh):
    return jax.shard_map(
        on_device,
        mesh=mesh,
        in_specs=(
            P(None, ("wide", "narrow"), None, None),
            P(None, ("wide", "narrow"), None, None),
            P(None, ("wide", "narrow")),
            P(),
            P(None, "narrow"),
            P(None, "narrow"),
            P("narrow", None),
            P("narrow", None),
            P("narrow", None),
            P("narrow", None),
            P(None, "narrow"),
            P("narrow"),
        ),
        out_specs=(
            P(None, ("wide", "narrow"), None, None),
            P(None, ("wide", "narrow"), None, None),
            P(None, "narrow"),
            P(None, "narrow"),
            P("narrow", None),
            P("narrow", None),
            P("narrow", None),
            P("narrow", None),
            P(None, "narrow"),
            P("narrow"),
        ),
        check_vma=False,
    )
```

profile of v0, /device:TPU:0, one launch (start us, length us, event | category | flops | bytes accessed | tf_op | source)
XLA Modules:
  0.0 1364.5 jit_solution(11387868374793793821)
XLA Ops:
  30.1 62.6 %all-gather.5.cloned.1.call-done = bf16[1024,3072]{1,0:T(8,128)(2,1)} async-done(((bf16[512,3072]{1,0:T(8,128)(2,1)}), bf16[1024,3072]{1,0:T(8,128)(2,1)}) %all-gather.5.cloned.1.call-update) | async-done | bytes 6291472 | tf_op jit(solution)/shard_map/all_gather | solution.py:199
  104.4 23.1 %all-gather.7.cloned.1.call-done = bf16[1024,1024]{1,0:T(8,128)(2,1)} async-done(((bf16[512,1024]{1,0:T(8,128)(2,1)}), bf16[1024,1024]{1,0:T(8,128)(2,1)}) %all-gather.7.cloned.1.call-update) | async-done | bytes 2097168 | tf_op jit(solution)/shard_map/all_gather | solution.py:200
  138.8 94.2 %all-gather.9.cloned.1.call-done = bf16[1024,4096]{1,0:T(8,128)(2,1)} async-done(((bf16[512,4096]{1,0:T(8,128)(2,1)}), bf16[1024,4096]{1,0:T(8,128)(2,1)}) %all-gather.9.cloned.1.call-update) | async-done | bytes 8388624 | tf_op jit(solution)/shard_map/all_gather | solution.py:201
  233.0 9.9 multiply_convert_fusion
  242.9 95.5 %all-gather.11.cloned.1.call-done = bf16[4096,1024]{1,0:T(8,128)(2,1)} async-done(((bf16[2048,1024]{1,0:T(8,128)(2,1)}), bf16[4096,1024]{1,0:T(8,128)(2,1)}) %all-gather.11.cloned.1.call-update) | async-done | bytes 8388624 | tf_op jit(solution)/shard_map/all_gather | solution.py:202
  344.5 9.1 multiply_convert_fusion.1
  420.1 7.1 convolution_convert_fusion.2
  427.2 7.2 convolution_convert_fusion.3
  470.9 62.1 %reduce-scatter.29.cloned.1.call-done = bf16[512,3072]{1,0:T(8,128)(2,1)} async-done(((bf16[1024,3072]{1,0:T(8,128)(2,1)}), bf16[512,3072]{1,0:T(8,128)(2,1)}) %reduce-scatter.29.cloned.1.call-update) | async-done | bytes 3145744 | tf_op jit(solution)/shard_map/reduce_scatter | solution.py:228
  533.0 79.5 %reduce-scatter.27.cloned.1.call-done = bf16[512,3072]{1,0:T(8,128)(2,1)} async-done(((bf16[1024,3072]{1,0:T(8,128)(2,1)}), bf16[512,3072]{1,0:T(8,128)(2,1)}) %reduce-scatter.27.cloned.1.call-update) | async-done | bytes 3145744 | tf_op jit(solution)/shard_map/reduce_scatter | solution.py:228
  618.2 96.6 %reduce-scatter.37.cloned.1.call-done = bf16[512,4096]{1,0:T(8,128)(2,1)} async-done(((bf16[1024,4096]{1,0:T(8,128)(2,1)}), bf16[512,4096]{1,0:T(8,128)(2,1)}) %reduce-scatter.37.cloned.1.call-update) | async-done | bytes 4194320 | tf_op jit(solution)/shard_map/reduce_scatter | solution.py:234
  714.7 102.1 %reduce-scatter.35.cloned.1.call-done = bf16[512,4096]{1,0:T(8,128)(2,1)} async-done(((bf16[1024,4096]{1,0:T(8,128)(2,1)}), bf16[512,4096]{1,0:T(8,128)(2,1)}) %reduce-scatter.35.cloned.1.call-update) | async-done | bytes 4194320 | tf_op jit(solution)/shard_map/reduce_scatter | solution.py:234
  816.8 7.2 add_convert_fusion.1
  824.1 94.4 %reduce-scatter.41.cloned.1.call-done = bf16[2048,1024]{1,0:T(8,128)(2,1)} async-done(((bf16[4096,1024]{1,0:T(8,128)(2,1)}), bf16[2048,1024]{1,0:T(8,128)(2,1)}) %reduce-scatter.41.cloned.1.call-update) | async-done | bytes 4194320 | tf_op jit(solution)/shard_map/reduce_scatter | solution.py:237
  918.5 101.5 %reduce-scatter.39.cloned.1.call-done = bf16[2048,1024]{1,0:T(8,128)(2,1)} async-done(((bf16[4096,1024]{1,0:T(8,128)(2,1)}), bf16[2048,1024]{1,0:T(8,128)(2,1)}) %reduce-scatter.39.cloned.1.call-update) | async-done | bytes 4194320 | tf_op jit(solution)/shard_map/reduce_scatter | solution.py:237
  1020.0 7.6 add_convert_fusion
  1029.5 6.9 all-reduce.4
  1039.5 8.4 reduce-scatter.43.cloned.1.call-done
  1048.9 12.9 reduce-scatter.49.cloned.1.call-done
  1062.8 12.9 reduce-scatter.47.cloned.1.call-done
  1076.7 12.9 reduce-scatter.53.cloned.1.call-done
  1090.5 12.9 reduce-scatter.51.cloned.1.call-done
  1104.5 64.5 %all-reduce.2 = (bf16[4,512]{1,0:T(4,128)(2,1)S(1)}, bf16[4,512]{1,0:T(4,128)(2,1)S(1)}, bf16[4,512]{1,0:T(4,128)(2,1)S(1)}, bf16[2048]{0:T(1024)(128)(2,1)S(1)}) all-reduce(bf16[4,512]{1,0:T(4,128)(2,1)S(1)} %add_convert_fusion.19, bf16[4,512]{1,0:T(4,128)(2,1)S(1)} %add_convert_fusion.18, ...), channel_id=1, replica_groups=mesh['wide'=16,'narrow'=2] {'wide'}, use_global_device_ids=true, to_apply=%region_49.50 | all-reduce | flops 8192 | bytes 32768 | tf_op jit(solution)/shard_map/psum | solution.py:252
  1171.4 170.0 %all-reduce.7.cloned.1.call-done = (bf16[512,3072]{1,0:T(8,128)(2,1)}, bf16[512,1024]{1,0:T(8,128)(2,1)}, bf16[512,4096]{1,0:T(8,128)(2,1)}, bf16[2048,1024]{1,0:T(8,128)(2,1)}) async-done(((bf16[512,3072]{1,0:T(8,128)(2,1)}, bf16[512,1024]{1,0:T(8,128)(2,1)}, bf16[512,4096]{1,0:T(8,128)(2,1)}, bf16[2048,1024]{1,0:T(8,128)(2,1)}), (bf16[512,3072]{1,0:T(8,128)(2,1)}, bf16[512,1024]{1,0:T(8,128)(2,1)}, ...) | async-done | bytes 12582928 | tf_op jit(solution)/shard_map/psum | solution.py:254
  (343 shorter events, 187.0 us)
Async XLA Ops:
  7.2 85.5 %all-gather.5.cloned.1.call-start = ((), (), s32[]{:S(2)}) async-start(), calls=%async_computation.14 | async-start | bytes 9437184 | tf_op jit(solution)/shard_map/all_gather | solution.py:199
  7.9 119.5 %all-gather.7.cloned.1.call-start = ((), (), s32[]{:S(2)}) async-start(), calls=%async_computation.15 | async-start | bytes 3145728 | tf_op jit(solution)/shard_map/all_gather | solution.py:200
  8.7 224.3 %all-gather.9.cloned.1.call-start = ((), (), s32[]{:S(2)}) async-start(), calls=%async_computation.16 | async-start | bytes 12582912 | tf_op jit(solution)/shard_map/all_gather | solution.py:201
  9.5 328.9 %all-gather.11.cloned.1.call-start = ((), (), s32[]{:S(2)}) async-start(), calls=%async_computation.17 | async-start | bytes 12582912 | tf_op jit(solution)/shard_map/all_gather | solution.py:202
  10.0 457.9 %reduce-scatter.33.cloned.1.call-start = ((), (), s32[]{:S(2)}) async-start(), calls=%async_computation.21 | async-start | bytes 3145728 | tf_op jit(solution)/shard_map/reduce_scatter | solution.py:231
  29.4 67.2 %copy-start.52 = (f32[128]{0:T(128)}, f32[128]{0:T(128)S(1)}, u32[]{:S(2)}) copy-start(f32[128]{0:T(128)S(1)} %get-tuple-element.41) | copy-start | bytes 1540
  101.5 30.6 %copy-start.20 = (bf16[128,3072]{0,1:T(8,128)(2,1)}, bf16[128,3072]{0,1:T(8,128)(2,1)S(1)}, u32[]{:S(2)}) copy-start(bf16[128,3072]{0,1:T(8,128)(2,1)S(1)} %copy.66) | copy-start | bytes 2359300
  104.4 27.7 %copy-start.34 = (bf16[16,64,128]{2,1,0:T(8,128)(2,1)}, bf16[16,64,128]{2,1,0:T(8,128)(2,1)S(1)}, u32[]{:S(2)}) copy-start(bf16[16,64,128]{2,1,0:T(8,128)(2,1)S(1)} %convolution_convert_fusion.11) | copy-start | bytes 786436
  137.0 105.9 %copy-start.56 = (f32[128]{0:T(128)}, f32[128]{0:T(128)S(1)}, u32[]{:S(2)}) copy-start(f32[128]{0:T(128)S(1)} %multiply_reduce_fusion.14) | copy-start | bytes 1540
  138.8 104.2 %copy-start.58 = (f32[128]{0:T(128)}, f32[128]{0:T(128)S(1)}, u32[]{:S(2)}) copy-start(f32[128]{0:T(128)S(1)} %multiply_reduce_fusion.16) | copy-start | bytes 1540
  386.9 81.1 %reduce-scatter.31.cloned.1.call-start = ((), (), s32[]{:S(2)}) async-start(), calls=%async_computation.20 | async-start | bytes 3145728 | tf_op jit(solution)/shard_map/reduce_scatter | solution.py:231
  391.1 141.9 %reduce-scatter.29.cloned.1.call-start = ((), (), s32[]{:S(2)}) async-start(), calls=%async_computation.19 | async-start | bytes 9437184 | tf_op jit(solution)/shard_map/reduce_scatter | solution.py:228
  407.5 205.0 %reduce-scatter.27.cloned.1.call-start = ((), (), s32[]{:S(2)}) async-start(), calls=%async_computation.18 | async-start | bytes 9437184 | tf_op jit(solution)/shard_map/reduce_scatter | solution.py:228
  419.1 295.7 %reduce-scatter.37.cloned.1.call-start = ((), (), s32[]{:S(2)}) async-start(), calls=%async_computation.23 | async-start | bytes 12582912 | tf_op jit(solution)/shard_map/reduce_scatter | solution.py:234
  427.2 389.6 %reduce-scatter.35.cloned.1.call-start = ((), (), s32[]{:S(2)}) async-start(), calls=%async_computation.22 | async-start | bytes 12582912 | tf_op jit(solution)/shard_map/reduce_scatter | solution.py:234
  434.5 484.0 %reduce-scatter.41.cloned.1.call-start = ((), (), s32[]{:S(2)}) async-start(), calls=%async_computation.25 | async-start | bytes 12582912 | tf_op jit(solution)/shard_map/reduce_scatter | solution.py:237
  441.3 578.7 %reduce-scatter.39.cloned.1.call-start = ((), (), s32[]{:S(2)}) async-start(), calls=%async_computation.24 | async-start | bytes 12582912 | tf_op jit(solution)/shard_map/reduce_scatter | solution.py:237
  448.2 590.3 %reduce-scatter.45.cloned.1.call-start = ((), (), s32[]{:S(2)}) async-start(), calls=%async_computation.27 | async-start | bytes 393216
  462.5 585.4 %reduce-scatter.43.cloned.1.call-start = ((), (), s32[]{:S(2)}) async-start(), calls=%async_computation.26 | async-start | bytes 393216
  463.5 598.3 %reduce-scatter.49.cloned.1.call-start = ((), (), s32[]{:S(2)}) async-start(), calls=%async_computation.29 | async-start | bytes 393216
  464.5 611.1 %reduce-scatter.47.cloned.1.call-start = ((), (), s32[]{:S(2)}) async-start(), calls=%async_computation.28 | async-start | bytes 393216
  465.7 623.8 %reduce-scatter.53.cloned.1.call-start = ((), (), s32[]{:S(2)}) async-start(), calls=%async_computation.31 | async-start | bytes 393216
  466.9 636.5 %reduce-scatter.51.cloned.1.call-start = ((), (), s32[]{:S(2)}) async-start(), calls=%async_computation.30 | async-start | bytes 393216
  467.9 873.5 %all-reduce.7.cloned.1.call-start = ((), (), s32[]{:S(2)}) async-start(), calls=%async_computation.32 | async-start | bytes 25165824 | tf_op jit(solution)/shard_map/psum | solution.py:254
  (60 other events, 282.4 us)
Sparse Core Ops, SparseCore 0:
  9.5 83.1 all-gather.4
  94.2 33.1 all-gather.6
  129.0 103.9 all-gather.8
  234.4 103.9 all-gather.10
  387.0 31.8 reduce-scatter.32
  421.0 31.8 reduce-scatter.30
  455.8 77.1 reduce-scatter.28
  535.3 77.1 reduce-scatter.26
  615.4 99.3 reduce-scatter.36
  717.4 99.3 reduce-scatter.34
  819.1 99.3 reduce-scatter.40
  920.6 99.3 reduce-scatter.38
  1022.2 11.7 reduce-scatter.44
  1036.1 11.7 reduce-scatter.42
  1050.0 11.7 reduce-scatter.48
  1063.9 11.7 reduce-scatter.46
  1077.7 11.7 reduce-scatter.52
  1091.6 11.7 reduce-scatter.50
  1108.6 232.8 all-reduce.6
where the time goes:
time: 1370 us; the launch traced here: 1360 us
  waiting for transfers between devices  1040 us (76%)
  matrix products  125 us (9%)
  blocking collectives  90 us (7%)
  other arithmetic  59 us (4%)
  local copies, waits for them, and re-layouts  28.8 us (2%)
  between operations  16.4 us (1%)
    reduce_scatter x2, waiting for transfers between devices, on_device(): lax.psum_scatter(grads[4].astype(jnp.bfloat16), 'narrow', scatter_dimensi...  199 us
    reduce_scatter x2, waiting for transfers between devices, on_device(): lax.psum_scatter(grads[5].astype(jnp.bfloat16), 'narrow', scatter_dimensi...  196 us
    psum x1, waiting for transfers between devices, on_device(): lax.psum(totals[2].astype(jnp.bfloat16), 'wide').astype(jnp.float32)  170 us
    reduce_scatter x2, waiting for transfers between devices, on_device(): lax.psum_scatter(grads[2].astype(jnp.bfloat16), 'narrow', scatter_dimensi...  142 us
    all_gather x1, waiting for transfers between devices, on_device(): lax.all_gather(w_down, 'narrow', axis=0, tiled=True)  95.5 us
    all_gather x1, waiting for transfers between devices, on_device(): lax.all_gather(w_up, 'narrow', axis=0, tiled=True)  94.2 us
    psum x1, blocking collectives, on_device(): lax.psum(totals[0].astype(jnp.bfloat16), 'wide').astype(jnp.float32)  64.5 us
    unnamed x25, waiting for transfers between devices  62.7 us
  transfers between devices with their start and end apart: 19, of which 16 were waited for; matrix products, arithmetic and copies ran while one was open for 10% of the time, Pallas kernels for 0%

commit v1 on v0

--- a/solution.py
+++ b/solution.py
@@ -7,6 +7,28 @@
 HEADS = 16
 EPSILON = 1e-05
 RELAX = 32.0
+
+
+def laid_out(tiles, dim):
+    tiles = jnp.moveaxis(tiles, 0, dim)
+    shape = tiles.shape
+    return tiles.reshape(*shape[:dim], shape[dim] * shape[dim + 1], *shape[dim + 2 :])
+
+
+def doubled(shard, axis):
+    devices = lax.axis_size(axis)
+    blocks = shard[None]
+    for level in range(devices.bit_length() - 1):
+        stride = 1 << level
+        received = lax.ppermute(blocks, axis, [(i, i ^ stride) for i in range(devices)])
+        both = jnp.stack([blocks, received])
+        upper = lax.axis_index(axis) >> level & 1
+        blocks = jnp.where(upper == 0, both, both[::-1]).reshape(-1, *shard.shape)
+    return blocks
+
+
+def gather_by_bits(value, axis, dim):
+    return laid_out(doubled(value, axis), dim)
 
 
 def layer_norm(value, gain, shift):
@@ -198,7 +220,7 @@
             lax.all_gather(norm_bias, "narrow", axis=1, tiled=True),
             lax.all_gather(w_qkv, "narrow", axis=0, tiled=True),
             lax.all_gather(w_out, "narrow", axis=0, tiled=True),
-            lax.all_gather(w_up, "narrow", axis=0, tiled=True),
+            gather_by_bits(w_up, "narrow", 0),
             lax.all_gather(w_down, "narrow", axis=0, tiled=True),
             lax.all_gather(bias_model, "narrow", axis=1, tiled=True),
             lax.all_gather(bias_up, "narrow", axis=0, tiled=True),

time: 1370 us -> 1420 us (1.036)
  blocking collectives: 90 us -> 243 us
  waiting for transfers between devices: 1040 us -> 889 us
  other arithmetic: 59 us -> 83 us
  matrix products: 125 us -> 143 us
    all_gather x1, blocking collectives: 4.36 us -> 158 us  [on_device(): lax.all_gather(bias_up, 'narrow', axis=0, tiled=True)]
    all_gather x1, waiting for transfers between devices: 62.6 us -> 0.01 us  [on_device(): lax.all_gather(w_qkv, 'narrow', axis=0, tiled=True)]
    all_gather x1, waiting for transfers between devices: 95.5 us -> 35.2 us  [on_device(): lax.all_gather(w_down, 'narrow', axis=0, tiled=True)]
    all_gather x1, waiting for transfers between devices: 23.1 us -> 0.02 us  [on_device(): lax.all_gather(w_out, 'narrow', axis=0, tiled=True)]
    dot_general x8, matrix products: 36.4 us -> 51.4 us  [forward_product(): return jnp.dot(left, right, preferred_element_type=jnp.float32)]
    select_n x0 -> x1, other arithmetic: none -> 14.6 us  [doubled(): blocks = jnp.where(upper == 0, both, both[::-1]).reshape(-1, *shard.shape)]
  transfers between devices with their start and end apart: 19 -> 20, of which waited for: 16 -> 14; matrix products, arithmetic and copies ran while one was open for 10% -> 15% of each run, Pallas kernels for 0% -> 0%
where the time goes in v1:
time: 1420 us; the launch traced here: 1410 us
  waiting for transfers between devices  889 us (63%)
  blocking collectives  243 us (17%)
  matrix products  143 us (10%)
  other arithmetic  83 us (6%)
  local copies, waits for them, and re-layouts  31 us (2%)
  between operations  16.3 us (1%)
    reduce_scatter x2, waiting for transfers between devices, on_device(): lax.psum_scatter(grads[4].astype(jnp.bfloat16), 'narrow', scatter_dimensi...  199 us
    reduce_scatter x2, waiting for transfers between devices, on_device(): lax.psum_scatter(grads[5].astype(jnp.bfloat16), 'narrow', scatter_dimensi...  196 us
    psum x1, waiting for transfers between devices, on_device(): lax.psum(totals[2].astype(jnp.bfloat16), 'wide').astype(jnp.float32)  170 us
    all_gather x1, blocking collectives, on_device(): lax.all_gather(bias_up, 'narrow', axis=0, tiled=True)  158 us
    reduce_scatter x2, waiting for transfers between devices, on_device(): lax.psum_scatter(grads[2].astype(jnp.bfloat16), 'narrow', scatter_dimensi...  141 us
    all_gather x1, waiting for transfers between devices, on_device(): lax.all_gather(w_up, 'narrow', axis=0, tiled=True)  86.3 us
    psum x1, blocking collectives, on_device(): lax.psum(totals[0].astype(jnp.bfloat16), 'wide').astype(jnp.float32)  64.1 us
    unnamed x25, waiting for transfers between devices  62.2 us
  transfers between devices with their start and end apart: 20, of which 14 were waited for; matrix products, arithmetic and copies ran while one was open for 15% of the time, Pallas kernels for 0%

profile of v1, /device:TPU:0, one launch (start us, length us, event | category | flops | bytes accessed | tf_op | source)
XLA Modules:
  0.0 1410.1 jit_solution(13239620144524256360)
XLA Ops:
  12.6 158.3 %all_gather.21 = bf16[4096]{0:T(1024)(128)(2,1)S(1)} all-gather(bf16[2048]{0:T(1024)(128)(2,1)S(1)} %copy-done.53), channel_id=1, replica_groups=mesh['wide'=16,'narrow'=2] {'narrow'}, dimensions={0}, use_global_device_ids=true | all-gather | bytes 12288 | tf_op jit(solution)/shard_map/all_gather | solution.py:226
  186.6 7.6 pad_maximum_fusion
  194.2 14.6 %reverse_select_fusion = bf16[2,1,512,4096]{3,2,1,0:T(8,128)(2,1)} fusion(bf16[2,1,512,4096]{3,2,1,0:T(8,128)(2,1)} %pad_maximum_fusion, pred[]{:T(512)S(6)} %eq.25), kind=kLoop, calls=%fused_computation.2 | loop fusion | flops 4194304 | bytes 16777216 | tf_op jit(solution)/shard_map/jit(_where)/select_n | solution.py:26
  234.2 22.5 %multiply_convert_fusion = (bf16[128,4096]{1,0:T(8,128)(2,1)}, f32[128,4096]{1,0:T(8,128)}, f32[128,4096]{1,0:T(8,128)}) fusion(f32[4096]{0:T(1024)S(1)} %convert_element_type.401, bf16[1024,4096]{1,0:T(8,128)(2,1)} %bitcast.294, f32[128,1024]{1,0:T(8,128)S(1)} %get-tuple-element.93, f32[128]{0:T(128)S(1)} %fusion.113, ...), kind=kOutput, calls=%fused_computation.26 | convolution fusion | flops 1109000192 | bytes 14181376 | tf_op jit(solution)/shard_map/dot_general | solution.py:46
  256.8 8.9 multiply_convert_fusion.1
  265.7 35.2 %all-gather.9.cloned.1.call-done = bf16[4096,1024]{1,0:T(8,128)(2,1)} async-done(((bf16[2048,1024]{1,0:T(8,128)(2,1)}), bf16[4096,1024]{1,0:T(8,128)(2,1)}) %all-gather.9.cloned.1.call-update) | async-done | bytes 8388624 | tf_op jit(solution)/shard_map/all_gather | solution.py:224
  320.0 86.3 %all-gather.11.cloned.1.call-done = bf16[1024,4096]{1,0:T(8,128)(2,1)} async-done(((bf16[512,4096]{1,0:T(8,128)(2,1)}), bf16[1024,4096]{1,0:T(8,128)(2,1)}) %all-gather.11.cloned.1.call-update) | async-done | bytes 8388624 | tf_op jit(solution)/shard_map/all_gather | solution.py:235
  413.1 7.0 fusion.125
  466.5 7.2 convolution_convert_fusion.2
  517.6 61.1 %reduce-scatter.29.cloned.1.call-done = bf16[512,3072]{1,0:T(8,128)(2,1)} async-done(((bf16[1024,3072]{1,0:T(8,128)(2,1)}), bf16[512,3072]{1,0:T(8,128)(2,1)}) %reduce-scatter.29.cloned.1.call-update) | async-done | bytes 3145744 | tf_op jit(solution)/shard_map/reduce_scatter | solution.py:250
  578.6 79.5 %reduce-scatter.27.cloned.1.call-done = bf16[512,3072]{1,0:T(8,128)(2,1)} async-done(((bf16[1024,3072]{1,0:T(8,128)(2,1)}), bf16[512,3072]{1,0:T(8,128)(2,1)}) %reduce-scatter.27.cloned.1.call-update) | async-done | bytes 3145744 | tf_op jit(solution)/shard_map/reduce_scatter | solution.py:250
  663.8 96.6 %reduce-scatter.37.cloned.1.call-done = bf16[512,4096]{1,0:T(8,128)(2,1)} async-done(((bf16[1024,4096]{1,0:T(8,128)(2,1)}), bf16[512,4096]{1,0:T(8,128)(2,1)}) %reduce-scatter.37.cloned.1.call-update) | async-done | bytes 4194320 | tf_op jit(solution)/shard_map/reduce_scatter | solution.py:256
  760.4 102.1 %reduce-scatter.35.cloned.1.call-done = bf16[512,4096]{1,0:T(8,128)(2,1)} async-done(((bf16[1024,4096]{1,0:T(8,128)(2,1)}), bf16[512,4096]{1,0:T(8,128)(2,1)}) %reduce-scatter.35.cloned.1.call-update) | async-done | bytes 4194320 | tf_op jit(solution)/shard_map/reduce_scatter | solution.py:256
  862.4 7.2 add_convert_fusion.1
  869.7 94.4 %reduce-scatter.41.cloned.1.call-done = bf16[2048,1024]{1,0:T(8,128)(2,1)} async-done(((bf16[4096,1024]{1,0:T(8,128)(2,1)}), bf16[2048,1024]{1,0:T(8,128)(2,1)}) %reduce-scatter.41.cloned.1.call-update) | async-done | bytes 4194320 | tf_op jit(solution)/shard_map/reduce_scatter | solution.py:259
  964.1 101.5 %reduce-scatter.39.cloned.1.call-done = bf16[2048,1024]{1,0:T(8,128)(2,1)} async-done(((bf16[4096,1024]{1,0:T(8,128)(2,1)}), bf16[2048,1024]{1,0:T(8,128)(2,1)}) %reduce-scatter.39.cloned.1.call-update) | async-done | bytes 4194320 | tf_op jit(solution)/shard_map/reduce_scatter | solution.py:259
  1065.6 7.6 add_convert_fusion
  1085.2 8.4 reduce-scatter.43.cloned.1.call-done
  1094.5 12.9 reduce-scatter.49.cloned.1.call-done
  1108.4 12.9 reduce-scatter.47.cloned.1.call-done
  1122.3 12.9 reduce-scatter.53.cloned.1.call-done
  1136.2 12.9 reduce-scatter.51.cloned.1.call-done
  1150.1 64.1 %all-reduce.2 = (bf16[4,512]{1,0:T(4,128)(2,1)S(1)}, bf16[4,512]{1,0:T(4,128)(2,1)S(1)}, bf16[4,512]{1,0:T(4,128)(2,1)S(1)}, bf16[2048]{0:T(1024)(128)(2,1)S(1)}) all-reduce(bf16[4,512]{1,0:T(4,128)(2,1)S(1)} %add_convert_fusion.19, bf16[4,512]{1,0:T(4,128)(2,1)S(1)} %add_convert_fusion.18, ...), channel_id=1, replica_groups=mesh['wide'=16,'narrow'=2] {'wide'}, use_global_device_ids=true, to_apply=%region_49.50 | all-reduce | flops 8192 | bytes 32768 | tf_op jit(solution)/shard_map/psum | solution.py:274
  1216.6 170.5 %all-reduce.7.cloned.1.call-done = (bf16[512,3072]{1,0:T(8,128)(2,1)}, bf16[512,1024]{1,0:T(8,128)(2,1)}, bf16[512,4096]{1,0:T(8,128)(2,1)}, bf16[2048,1024]{1,0:T(8,128)(2,1)}) async-done(((bf16[512,3072]{1,0:T(8,128)(2,1)}, bf16[512,1024]{1,0:T(8,128)(2,1)}, bf16[512,4096]{1,0:T(8,128)(2,1)}, bf16[2048,1024]{1,0:T(8,128)(2,1)}), (bf16[512,3072]{1,0:T(8,128)(2,1)}, bf16[512,1024]{1,0:T(8,128)(2,1)}, ...) | async-done | bytes 12582928 | tf_op jit(solution)/shard_map/psum | solution.py:276
  (370 shorter events, 201.8 us)
Async XLA Ops:
  7.2 201.6 %all-gather.5.cloned.1.call-start = ((), (), s32[]{:S(2)}) async-start(), calls=%async_computation.14 | async-start | bytes 9437184 | tf_op jit(solution)/shard_map/all_gather | solution.py:221
  7.9 217.7 %all-gather.7.cloned.1.call-start = ((), (), s32[]{:S(2)}) async-start(), calls=%async_computation.15 | async-start | bytes 3145728 | tf_op jit(solution)/shard_map/all_gather | solution.py:222
  8.7 292.2 %all-gather.9.cloned.1.call-start = ((), (), s32[]{:S(2)}) async-start(), calls=%async_computation.16 | async-start | bytes 12582912 | tf_op jit(solution)/shard_map/all_gather | solution.py:224
  9.4 396.9 %all-gather.11.cloned.1.call-start = ((), (), s32[]{:S(2)}) async-start(), calls=%async_computation.17 | async-start | bytes 12582912 | tf_op jit(solution)/shard_map/all_gather | solution.py:235
  9.5 170.6 %copy-start.56 = (bf16[4,512]{1,0:T(4,128)(2,1)S(1)}, bf16[4,512]{1,0:T(4,128)(2,1)}, u32[]{:S(2)}) copy-start(bf16[4,512]{1,0:T(4,128)(2,1)} %param.16) | copy-start | bytes 12292
  9.5 175.1 %copy-start.65 = (s32[16]{0:T(128)S(1)}, s32[16]{0:T(128)}, u32[]{:S(2)}) copy-start(s32[16]{0:T(128)} %param.15) | copy-start | bytes 196
  9.5 175.1 %copy-start.66 = (s32[2,1]{0,1:T(1,128)S(1)}, s32[2,1]{0,1:T(1,128)}, u32[]{:S(2)}) copy-start(s32[2,1]{0,1:T(1,128)} %param.14) | copy-start | bytes 28
  9.5 176.1 %copy-start.2 = (bf16[2,1,128,1024]{3,2,1,0:T(8,128)(2,1)S(1)}, bf16[2,1,128,1024]{3,2,1,0:T(8,128)(2,1)}, u32[]{:S(2)}) copy-start(bf16[2,1,128,1024]{3,2,1,0:T(8,128)(2,1)} %param.12) | copy-start | bytes 1572868
  9.5 177.1 %collective-permute-start = (bf16[1,512,4096]{2,1,0:T(8,128)(2,1)}, bf16[1,512,4096]{2,1,0:T(8,128)(2,1)}, u32[]{:S(2)}, u32[]{:S(2)}) collective-permute-start(bf16[1,512,4096]{2,1,0:T(8,128)(2,1)} %bitcast.292), channel_id=1, source_target_pairs={{0,1},{1,0},{2,3},{3,2},{4,5},{5,4},{6,7},{7,6},{8,9},{9,8},{10,11... | collective-permute-start | bytes 12582920 | tf_op jit(solution)/shard_map/ppermute | solution.py:23
  12.6 502.1 %reduce-scatter.33.cloned.1.call-start = ((), (), s32[]{:S(2)}) async-start(), calls=%async_computation.21 | async-start | bytes 3145728 | tf_op jit(solution)/shard_map/reduce_scatter | solution.py:253
  432.5 82.2 %reduce-scatter.31.cloned.1.call-start = ((), (), s32[]{:S(2)}) async-start(), calls=%async_computation.20 | async-start | bytes 3145728 | tf_op jit(solution)/shard_map/reduce_scatter | solution.py:253
  436.8 141.9 %reduce-scatter.29.cloned.1.call-start = ((), (), s32[]{:S(2)}) async-start(), calls=%async_computation.19 | async-start | bytes 9437184 | tf_op jit(solution)/shard_map/reduce_scatter | solution.py:250
  453.0 205.1 %reduce-scatter.27.cloned.1.call-start = ((), (), s32[]{:S(2)}) async-start(), calls=%async_computation.18 | async-start | bytes 9437184 | tf_op jit(solution)/shard_map/reduce_scatter | solution.py:250
  465.5 294.9 %reduce-scatter.37.cloned.1.call-start = ((), (), s32[]{:S(2)}) async-start(), calls=%async_computation.23 | async-start | bytes 12582912 | tf_op jit(solution)/shard_map/reduce_scatter | solution.py:256
  473.7 388.7 %reduce-scatter.35.cloned.1.call-start = ((), (), s32[]{:S(2)}) async-start(), calls=%async_computation.22 | async-start | bytes 12582912 | tf_op jit(solution)/shard_map/reduce_scatter | solution.py:256
  480.8 483.3 %reduce-scatter.41.cloned.1.call-start = ((), (), s32[]{:S(2)}) async-start(), calls=%async_computation.25 | async-start | bytes 12582912 | tf_op jit(solution)/shard_map/reduce_scatter | solution.py:259
  487.7 578.0 %reduce-scatter.39.cloned.1.call-start = ((), (), s32[]{:S(2)}) async-start(), calls=%async_computation.24 | async-start | bytes 12582912 | tf_op jit(solution)/shard_map/reduce_scatter | solution.py:259
  494.5 589.6 %reduce-scatter.45.cloned.1.call-start = ((), (), s32[]{:S(2)}) async-start(), calls=%async_computation.27 | async-start | bytes 393216
  508.9 584.6 %reduce-scatter.43.cloned.1.call-start = ((), (), s32[]{:S(2)}) async-start(), calls=%async_computation.26 | async-start | bytes 393216
  509.9 597.5 %reduce-scatter.49.cloned.1.call-start = ((), (), s32[]{:S(2)}) async-start(), calls=%async_computation.29 | async-start | bytes 393216
  511.0 610.3 %reduce-scatter.47.cloned.1.call-start = ((), (), s32[]{:S(2)}) async-start(), calls=%async_computation.28 | async-start | bytes 393216
  512.2 623.0 %reduce-scatter.53.cloned.1.call-start = ((), (), s32[]{:S(2)}) async-start(), calls=%async_computation.31 | async-start | bytes 393216
  513.3 635.7 %reduce-scatter.51.cloned.1.call-start = ((), (), s32[]{:S(2)}) async-start(), calls=%async_computation.30 | async-start | bytes 393216
  514.3 872.7 %all-reduce.7.cloned.1.call-start = ((), (), s32[]{:S(2)}) async-start(), calls=%async_computation.32 | async-start | bytes 25165824 | tf_op jit(solution)/shard_map/psum | solution.py:276
  (72 other events, 739.2 us)
Sparse Core Ops, SparseCore 0:
  9.5 150.5 all-gather.4
  161.7 33.3 all-gather.6
  196.6 104.2 all-gather.8
  302.3 103.9 all-gather.10
  432.6 31.8 reduce-scatter.32
  466.7 31.8 reduce-scatter.30
  501.5 77.1 reduce-scatter.28
  580.9 77.1 reduce-scatter.26
  661.0 99.3 reduce-scatter.36
  763.1 99.3 reduce-scatter.34
  864.7 99.3 reduce-scatter.40
  966.2 99.3 reduce-scatter.38
  1067.8 11.7 reduce-scatter.44
  1081.7 11.7 reduce-scatter.42
  1095.6 11.7 reduce-scatter.48
  1109.5 11.7 reduce-scatter.46
  1123.4 11.7 reduce-scatter.52
  1137.2 11.7 reduce-scatter.50
  1154.2 232.8 all-reduce.6
